TPU v7x, 128 devices: a whole 4x4x4 slice. The times are simulated.
128 devices in a mesh: comp: 4 (over x), dom: 32 (over y, z, core).
Axes of the slice: x: 4, y: 4, z: 4, core: 2. Of those that a mesh axis runs over, the one named last changes fastest.
Arguments:
- atm_state: float32 [4, 4, 128, 16, 4096], P('comp', None, None, None, 'dom'), may hold values from -6 to 6
- elem_nbr: int32 [4, 4, 4096], P('comp', None, 'dom'), may hold values from 0 to 12287, as said below
- elem_metric: float32 [4, 16, 4096], P('comp', None, 'dom'), may hold values from 0.02 to 0.2
- bulk_coef: float32 [4, 16, 4096], P('comp', None, 'dom'), may hold values from 0.2 to 2
- stiffness: float32 [16, 16], replicated, may hold values from -1.5 to 1.5
- coupling: float32 [4, 16, 16], replicated, may hold values from -1.5 to 1.5
- atm_vertical: float32 [128, 128], replicated, may hold values from -0.25 to 0.25
- ocean_state: float32 [4, 4, 80, 32768], P('comp', None, None, 'dom'), may hold values from -6 to 6
- cell_nbr: int32 [4, 6, 32768], P('comp', None, 'dom'), may hold values from 0 to 32767, as said below
- cell_diff: float32 [4, 6, 32768], P('comp', None, 'dom'), may hold values from 0.01 to 0.12
- ocean_vertical: float32 [80, 80], replicated, may hold values from -0.3125 to 0.3125
- sea_mask: int32 [4, 32768], P('comp', 'dom'), may hold values 0 or 1
- pair_owner: int32 [4, 1024, 1], P('comp', 'dom'), may hold values from 0 to 31, as said below
- pair_block: int32 [4, 1024], P('comp', 'dom'), may hold values from 0 to 7
- pair_src: int32 [4, 1024], P('comp', 'dom'), may hold values from 0 to 15
- remap_weight: float32 [4, 1024, 128, 128], P('comp', 'dom'), may hold values from -0.5 to 0.5
Outputs:
- atm_next: float32 [4, 4, 128, 16, 4096], P('comp', None, None, None, 'dom')
- ocean_next: float32 [4, 4, 80, 32768], P('comp', None, None, 'dom')
Inputs may be any that keep to these rules, and one draw needn't show every extreme that they name: `elem_nbr`: each entry of the slabs c < 3 differs from its own element index c * 4096 + e by 1 to 8; the last slab repeats the first. `cell_nbr`: each entry differs from its own cell index by 1 to 128; all slabs are equal. `pair_owner`: within the rows of one device (aligned blocks of 32 rows) no owner is named by more than 2 rows; the owners one below and one above that device's index of dom (counted round) are each named by exactly 2 rows.
All inputs are finite; a program needn't handle non-finite values. No bound on the sum of `sea_mask` on one device may be relied on, other than what follows from the above.
Results may differ from a plain program's by a relative error of at most 0.0001.
Values sent between devices are 32-bit elements; how exact they have to be, the bound alone decides.
A program may use at most 128 MiB of HBM per device.

v0:
```python
import functools

import jax
import jax.numpy as jnp
from jax import lax
from jax.experimental import pallas as pl
from jax.experimental.pallas import tpu as pltpu
from jax.sharding import PartitionSpec as P

f32, bf16, i32 = jnp.float32, jnp.bfloat16, jnp.int32
FIELDS, LEV, NPTS, ELEMS = 4, 128, 16, 128
ROWS = FIELDS * LEV
BLOCKS, WIDTH = 8, 16
LANES = NPTS * WIDTH
SLABS, DOM = 4, 32
ATM = SLABS - 1
PAIRS, BLK = 32, 128
OLEV, CELLS, NBR_O = 80, 1024, 6
OROWS = FIELDS * OLEV
OBLOCKS = CELLS // BLK
MESH = pl.DeviceIdType.MESH
highest = lax.Precision.HIGHEST


def iota(shape, axis):
    return lax.broadcasted_iota(i32, shape, axis)


def swap_chunks(a):
    chunk = iota(a[0].shape, 1) // WIDTH
    a = [a[q] if q == 0 else pltpu.roll(a[q], WIDTH * q, 1) for q in range(8)]
    for k in (1, 2, 4):
        take = (chunk & k) != 0
        a = [jnp.where(take, a[(i + k) % 8], a[i]) for i in range(8)]
    out = [a[(-b) % 8] for b in range(8)]
    return [out[b] if b == 0 else pltpu.roll(out[b], 128 - WIDTH * b, 1) for b in range(8)]


def split(x):
    hi = x.astype(bf16)
    return hi, (x - hi.astype(f32)).astype(bf16)


def pick_rows(onehot, x):
    hi, lo = split(x)
    return jnp.dot(onehot, hi, preferred_element_type=f32) + jnp.dot(
        onehot, lo, preferred_element_type=f32
    )


def pack(f, st, x, xh, xl):
    def body(i, _):
        row = f * LEV + i * 16
        for h in range(2):
            a = [st[pl.ds(row * NPTS + h * 8 + q, 16, stride=NPTS), :] for q in range(8)]
            w = swap_chunks(a)
            cols = slice(h * 128, (h + 1) * 128)
            for b in range(BLOCKS):
                hi, lo = split(w[b])
                x[b, pl.ds(row, 16), cols] = w[b]
                xh[b + 1, pl.ds(row, 16), cols] = hi
                xl[b + 1, pl.ds(row, 16), cols] = lo
        return 0

    lax.fori_loop(0, LEV // 16, body, 0, unroll=2)


def unpack(f, x, st):
    def body(i, _):
        row = f * LEV + i * 16
        for h in range(2):
            cols = slice(h * 128, (h + 1) * 128)
            w = swap_chunks([x[b, pl.ds(row, 16), cols] for b in range(BLOCKS)])
            for q in range(8):
                st[pl.ds(row * NPTS + h * 8 + q, 16, stride=NPTS), :] = w[q]
        return 0

    lax.fori_loop(0, LEV // 16, body, 0, unroll=2)


def small_tables(first, nbr, metric, stiff, coup, vert, cr, met, near, vv):
    spread = (iota((NPTS, LANES), 0) == iota((NPTS, LANES), 1) // WIDTH).astype(f32)
    for s in range(5):
        mat = coup[s] if s < 4 else stiff[...]
        cr[s] = lax.dot_general(
            mat, spread, (((0,), (0,)), ((), ())), precision=highest, preferred_element_type=f32
        )
    for h in range(2):
        w = swap_chunks(
            [jnp.broadcast_to(metric[h * 8 + q : h * 8 + q + 1, :], (8, 128)) for q in range(8)]
        )
        for b in range(BLOCKS):
            met[b, :, h * 128 : (h + 1) * 128] = w[b]
    own = jnp.concatenate([nbr[...], nbr[...]], axis=0) - first
    w = swap_chunks([own] * 8)
    for b in range(BLOCKS):
        near[b] = w[b] - b * WIDTH
    hi, lo = split(vert[...])
    vv[:LEV, :LEV] = hi
    vv[:LEV, LEV:] = hi
    vv[LEV:, :LEV] = lo
    vv[LEV:, LEV:] = jnp.zeros((LEV, LEV), bf16)


def operator_block(b, near, cr, th, tl):
    sub, lane = iota((WIDTH, LANES), 0), iota((WIDTH, LANES), 1)
    rows = near[b]
    inner, outer = [], []
    for s in range(4):
        r = rows[s : s + 1, :]
        r = jnp.concatenate([r, r], axis=1)
        hit = sub == jnp.broadcast_to(r & (WIDTH - 1), (WIDTH, LANES))
        inside = jnp.broadcast_to((r >= 0) & (r < WIDTH), (WIDTH, LANES))
        inner.append(hit & inside)
        outer.append(hit & jnp.logical_not(inside))
    diag = sub == (lane & (WIDTH - 1))
    for q in range(NPTS):
        vals = [jnp.broadcast_to(cr[s, q : q + 1, :], (WIDTH, LANES)) for s in range(5)]
        c = jnp.where(diag, vals[4], 0.0)
        d = jnp.zeros((WIDTH, LANES), f32)
        for s in range(4):
            c = c + jnp.where(inner[s], vals[s], 0.0)
            d = d + jnp.where(outer[s], vals[s], 0.0)
        for base, part in ((0, c), (LANES, d)):
            hi, lo = split(part)
            here = slice(base + q * WIDTH, base + (q + 1) * WIDTH)
            th[b, here, :] = hi
            tl[b, here, :] = lo


def advance(b, x, xh, xl, y, yh, yl, vv, th, tl, met):
    low = (iota((ROWS, LANES), 1) & (WIDTH - 1)) < WIDTH // 2
    sh = jnp.where(low, xh[b + 2], xh[b])
    sl = jnp.where(low, xl[b + 2], xl[b])
    ch, cl = xh[b + 1], xl[b + 1]
    lhs = jnp.concatenate([ch, sh, cl, sl, ch, sh], axis=1)
    rhs = jnp.concatenate([th[b], th[b], tl[b]], axis=0)
    acc = jnp.dot(lhs, rhs, preferred_element_type=f32)
    for f in range(FIELDS):
        g = slice(f * LEV, (f + 1) * LEV)
        parts = jnp.concatenate([xh[b + 1, g], xl[b + 1, g]], axis=0)
        v = jnp.dot(vv[...], parts, preferred_element_type=f32)
        new = x[b, g] + met[b, 0:1, :] * (acc[g] + v[:LEV] + v[LEV:])
        y[b, g] = new
        if yh is not None:
            hi, lo = split(new)
            yh[b + 1, g] = hi
            yl[b + 1, g] = lo


def add_surface(delta, y, yh, yl):
    last = iota((16, LANES), 0) == 15

    def body(b, _):
        for f in range(FIELDS):
            g = slice((f + 1) * LEV - 16, (f + 1) * LEV)
            new = y[b, g] + jnp.where(
                last, jnp.broadcast_to(delta[b, f : f + 1, :], (16, LANES)), 0.0
            )
            y[b, g] = new
            if yh is not None:
                hi, lo = split(new)
                yh[b + 1, g] = hi
                yl[b + 1, g] = lo
        return 0

    lax.fori_loop(0, BLOCKS, body, 0)


def edges_out(x, es):
    low = (iota((ROWS, 128), 1) & (WIDTH - 1)) < WIDTH // 2
    top = x[BLOCKS - 1]
    es[0] = jnp.where(low, pltpu.roll(top[:, 128:], 120, 1), top[:, :128])
    bottom = x[0]
    es[1] = jnp.where(low, bottom[:, :128], pltpu.roll(bottom[:, 128:], 8, 1))


def edges_in(er, xh, xl):
    for side, block, turn in ((0, 0, 8), (1, BLOCKS + 1, 120)):
        v = er[side]
        for cols, part in ((slice(0, 128), v), (slice(128, 256), pltpu.roll(v, turn, 1))):
            hi, lo = split(part)
            xh[block, :, cols] = hi
            xl[block, :, cols] = lo


def pair_tables(owner, block, src, slot_of, slot_to, point_of, point_to, ids):
    pair, col = iota((PAIRS, 256), 0), iota((PAIRS, 256), 1) // 8

    def over_columns(column):
        return jnp.sum(jnp.where(pair == col, column, 0.0), axis=0, keepdims=True)

    eye = iota((PAIRS, PAIRS), 0) == iota((PAIRS, PAIRS), 1)

    def as_column(row):
        wide = jnp.broadcast_to(row.astype(f32), (PAIRS, PAIRS))
        return jnp.sum(jnp.where(eye, wide, 0.0), axis=1, keepdims=True)

    own = jnp.broadcast_to(owner[...].astype(f32), (PAIRS, 256))
    own_c = over_columns(own)
    rank_c = jnp.sum(jnp.where((own == own_c) & (pair < col), 1.0, 0.0), axis=0, keepdims=True)
    slot_c = 2.0 * own_c + rank_c
    block_c = over_columns(jnp.broadcast_to(as_column(block[...]), (PAIRS, 256)))
    src_c = over_columns(jnp.broadcast_to(as_column(src[...]), (PAIRS, 256)))
    r, c = iota((256, 256), 0), iota((256, 256), 1)
    hit = ((r // 4).astype(f32) == slot_c) & ((r & 3) == (c & 7))
    table = hit.astype(f32)
    slot_of[...] = table.astype(bf16)
    slot_to[...] = table.T.astype(bf16)
    number = jnp.sum(table * (block_c + 1.0), axis=1, keepdims=True) - 1.0
    ids[...] = jnp.broadcast_to(number.astype(i32), (256, BLK)).reshape(DOM, 8, BLK)
    r, c = iota((64, 256), 0), iota((64, 256), 1)
    hit = ((r & 15).astype(f32) == src_c) & ((r // 16) == (c & 7))
    table = hit.astype(f32)
    point_of[...] = table.astype(bf16)
    point_to[...] = table.T.astype(bf16)


def pair_products(rows, wh, wl, out, transposed):
    dims = (((1,), (1 if transposed else 0,)), ((), ()))

    def body(i, _):
        for k in range(8):
            j = i * 8 + k
            v = rows[pl.ds(j * 8, 8), :]
            both = jnp.concatenate([v, v - v.astype(bf16).astype(f32)], axis=0).astype(bf16)
            a = lax.dot_general(both, wh[j], dims, preferred_element_type=f32)
            b = lax.dot_general(both, wl[j], dims, preferred_element_type=f32)
            out[pl.ds(j * 8, 8), :] = a[:8] + a[8:] + b[:8]
        return 0

    lax.fori_loop(0, PAIRS // 8, body, 0)


def kernel(
    state_hbm, weight_hbm, ocean_hbm, nbr, metric, coef, stiff, coup, vert,
    cell_nbr, cell_diff, overt, mask, owner, block, src,
    atm_hbm, ocean_out_hbm,
    st, x, xh, xl, y, yh, yl, vv, th, tl, met, cr, near, delta, flux,
    wt, wh, wl, rows_a, rows_b, slot_of, slot_to, point_of, point_to,
    es, er, es2, er2,
    ids_s, ids_r, rep_s, rep_r, flx_s, flx_r, surf_s, surf_r, ofl_s, ofl_r,
    oe, ob,
    st_sem, wt_sem, oc_sem, out_sem, zero_sem,
    ids_ss, ids_rs, rep_ss, rep_rs, flx_ss, flx_rs,
    surf_ss, surf_rs, ofl_ss, ofl_rs,
    edge_ss, edge_rs, edge2_ss, edge2_rs, oh_ss, oh_rs,
):
    c, d = lax.axis_index("comp"), lax.axis_index("dom")
    barrier = pltpu.get_barrier_semaphore()
    ocean_slab = SLABS - 1

    def remote(src_ref, dst_ref, send, recv, comp, dom):
        return pltpu.make_async_remote_copy(
            src_ref=src_ref, dst_ref=dst_ref, send_sem=send, recv_sem=recv,
            device_id=(comp, dom), device_id_type=MESH,
        )

    def greet(comp, dom):
        pl.semaphore_signal(barrier, inc=1, device_id=(comp, dom), device_id_type=MESH)

    @pl.when(c < ATM)
    def _atmosphere():
        state_in = [
            pltpu.make_async_copy(
                state_hbm.at[pl.ds(f * 2048, 2048)], st.at[pl.ds(f * 2048, 2048)], st_sem.at[f]
            )
            for f in range(FIELDS)
        ]
        for copy in state_in:
            copy.start()
        weights_in = pltpu.make_async_copy(weight_hbm, wt, wt_sem)
        weights_in.start()
        has_prev, has_next = (c + d) > 0, (c * DOM + d) < ATM * DOM - 1
        prev_c, prev_d = jnp.where(d == 0, c - 1, c), lax.rem(d + DOM - 1, DOM)
        next_c, next_d = jnp.where(d == DOM - 1, c + 1, c), lax.rem(d + 1, DOM)

        def other(i):
            return lax.rem(d + i, DOM)

        def hello(i, _):
            greet(c, other(i))
            return 0

        lax.fori_loop(1, DOM, hello, 0)
        greet(ocean_slab, d)
        cross_prev = (d == 0) & (c > 0)
        cross_next = (d == DOM - 1) & (c < ATM - 1)

        @pl.when(cross_prev)
        def _():
            greet(prev_c, prev_d)

        @pl.when(cross_next)
        def _():
            greet(next_c, next_d)

        pair_tables(owner, block, src, slot_of, slot_to, point_of, point_to, ids_s)
        pl.semaphore_wait(
            barrier, DOM + jnp.where(cross_prev, 1, 0) + jnp.where(cross_next, 1, 0)
        )

        def exchange(out, into, send, recv):
            def copy(i):
                o = other(i)
                return o, remote(out.at[o], into.at[d], send.at[o], recv.at[d], c, o)

            def start():
                def body(i, _):
                    copy(i)[1].start()
                    return 0

                into[d] = out[d]
                lax.fori_loop(1, DOM, body, 0)

            def arrive():
                def body(i, _):
                    o = other(i)
                    remote(out.at[o], into.at[o], send.at[o], recv.at[o], c, o).wait_recv()
                    return 0

                lax.fori_loop(1, DOM, body, 0)

            def sent():
                def body(i, _):
                    copy(i)[1].wait_send()
                    return 0

                lax.fori_loop(1, DOM, body, 0)

            return start, arrive, sent

        ids_start, ids_arrive, ids_sent = exchange(ids_s, ids_r, ids_ss, ids_rs)
        rep_start, rep_arrive, rep_sent = exchange(rep_s, rep_r, rep_ss, rep_rs)
        flx_start, flx_arrive, flx_sent = exchange(flx_s, flx_r, flx_ss, flx_rs)
        ids_start()

        def edge_copies(out, into, send, recv):
            up = remote(out.at[0], into.at[0], send.at[0], recv.at[0], next_c, next_d)
            down = remote(out.at[1], into.at[1], send.at[1], recv.at[1], prev_c, prev_d)

            def start():
                @pl.when(has_next)
                def _():
                    up.start()

                @pl.when(has_prev)
                def _():
                    down.start()

                @pl.when(jnp.logical_not(has_prev))
                def _():
                    into[0] = jnp.zeros((ROWS, 128), f32)

                @pl.when(jnp.logical_not(has_next))
                def _():
                    into[1] = jnp.zeros((ROWS, 128), f32)

            def arrive():
                @pl.when(has_prev)
                def _():
                    up.wait_recv()

                @pl.when(has_next)
                def _():
                    down.wait_recv()

            def sent():
                @pl.when(has_next)
                def _():
                    up.wait_send()

                @pl.when(has_prev)
                def _():
                    down.wait_send()

            return start, arrive, sent

        edge_start, edge_arrive, edge_sent = edge_copies(es, er, edge_ss, edge_rs)
        edge2_start, edge2_arrive, edge2_sent = edge_copies(es2, er2, edge2_ss, edge2_rs)

        for f in range(FIELDS):
            state_in[f].wait()
            pack(f, st, x, xh, xl)
        edges_out(x, es)
        edge_start()

        small_tables(c * (DOM * ELEMS) + d * ELEMS, nbr, metric, stiff, coup, vert, cr, met, near, vv)

        def table(b, _):
            operator_block(b, near, cr, th, tl)
            return 0

        lax.fori_loop(0, BLOCKS, table, 0)

        remote(surf_s, surf_r, surf_ss.at[0], surf_rs, ocean_slab, d).wait_recv()
        ids_arrive()

        def answer(i, _):
            which = ids_r[i]
            acc = jnp.zeros((8, BLK), f32)
            for b in range(OBLOCKS):
                acc = acc + jnp.where(which == b, surf_r[:, b * BLK : (b + 1) * BLK], 0.0)
            rep_s[i] = acc
            return 0

        lax.fori_loop(0, DOM, answer, 0, unroll=4)
        rep_start()

        weights_in.wait()

        def halves(j, _):
            hi, lo = split(wt[j])
            wh[j] = hi
            wl[j] = lo
            return 0

        lax.fori_loop(0, PAIRS, halves, 0, unroll=2)

        def first(i, _):
            @pl.when(i == BLOCKS - 2)
            def _():
                edge_arrive()
                edges_in(er, xh, xl)

            b = jnp.where(i < BLOCKS - 2, i + 1, (i - (BLOCKS - 2)) * (BLOCKS - 1))
            advance(b, x, xh, xl, y, yh, yl, vv, th, tl, met)
            return 0

        lax.fori_loop(0, BLOCKS, first, 0)

        rep_arrive()
        rows_a[...] = pick_rows(slot_to[...], rep_r[...].reshape(256, BLK))
        pair_products(rows_a, wh, wl, rows_b, True)
        surface = pick_rows(point_of[...], rows_b[...])
        top = jnp.concatenate(
            [st[f * 2048 + 2032 : f * 2048 + 2048, :] for f in range(FIELDS)], axis=0
        )
        fl = jnp.concatenate([coef[...]] * FIELDS, axis=0) * (top - surface)
        rows_a[...] = pick_rows(point_to[...], fl)
        pair_products(rows_a, wh, wl, rows_b, False)
        flx_s[...] = pick_rows(slot_of[...], rows_b[...]).reshape(DOM, 8, BLK)
        flx_start()

        flux[:64] = fl * -0.5
        flux[64:] = jnp.zeros((64, BLK), f32)
        for h in range(2):
            w = swap_chunks([flux[pl.ds(h * 8 + q, 8, stride=NPTS), :] for q in range(8)])
            for b in range(BLOCKS):
                delta[b, :, h * 128 : (h + 1) * 128] = w[b]
        add_surface(delta, y, yh, yl)
        edges_out(y, es2)
        edge2_start()

        def second(i, _):
            @pl.when(i == BLOCKS - 2)
            def _():
                edge2_arrive()
                edges_in(er2, yh, yl)
                flx_arrive()

                def gather(j, accs):
                    which, val = ids_r[j], flx_r[j]
                    return tuple(
                        acc + jnp.where(which == b, val, 0.0) for b, acc in enumerate(accs)
                    )

                zero = jnp.zeros((8, BLK), f32)
                accs = lax.fori_loop(0, DOM, gather, (zero,) * OBLOCKS, unroll=4)
                for b in range(OBLOCKS):
                    ofl_s[:, b * BLK : (b + 1) * BLK] = accs[b]
                remote(ofl_s, ofl_r.at[c], ofl_ss, ofl_rs.at[c], ocean_slab, d).start()

            b = jnp.where(i < BLOCKS - 2, i + 1, (i - (BLOCKS - 2)) * (BLOCKS - 1))
            advance(b, y, yh, yl, x, None, None, vv, th, tl, met)
            return 0

        lax.fori_loop(0, BLOCKS, second, 0)
        add_surface(delta, x, None, None)

        ob[...] = jnp.zeros((OROWS, CELLS), f32)
        zero_out = pltpu.make_async_copy(ob, ocean_out_hbm, zero_sem)
        zero_out.start()
        outs = [
            pltpu.make_async_copy(
                st.at[pl.ds(f * 2048, 2048)], atm_hbm.at[pl.ds(f * 2048, 2048)], out_sem.at[f]
            )
            for f in range(FIELDS)
        ]
        for f in range(FIELDS):
            unpack(f, x, st)
            outs[f].start()
        ids_sent()
        rep_sent()
        flx_sent()
        edge_sent()
        edge2_sent()
        remote(ofl_s, ofl_r.at[c], ofl_ss, ofl_rs.at[c], ocean_slab, d).wait_send()
        zero_out.wait()
        for copy in outs:
            copy.wait()

    @pl.when(c == ocean_slab)
    def _ocean():
        mid = oe.at[:, pl.ds(BLK, CELLS)]
        ocean_in = pltpu.make_async_copy(ocean_hbm, mid, oc_sem)
        ocean_in.start()
        for comp in range(ATM):
            greet(comp, d)
        has_prev, has_next = d > 0, d < DOM - 1

        @pl.when(has_prev)
        def _():
            greet(c, d - 1)

        @pl.when(has_next)
        def _():
            greet(c, d + 1)

        ocean_in.wait()
        for k in range(2):
            for f in range(FIELDS):
                surf_s[k * 4 + f : k * 4 + f + 1, :] = oe[f * OLEV : f * OLEV + 1, BLK : BLK + CELLS]
        pl.semaphore_wait(
            barrier, ATM + jnp.where(has_prev, 1, 0) + jnp.where(has_next, 1, 0)
        )
        surf_out = [
            remote(surf_s, surf_r, surf_ss.at[comp], surf_rs, comp, d) for comp in range(ATM)
        ]
        for copy in surf_out:
            copy.start()
        up = remote(
            oe.at[:, pl.ds(CELLS, BLK)], oe.at[:, pl.ds(0, BLK)],
            oh_ss.at[0], oh_rs.at[0], c, lax.rem(d + 1, DOM),
        )
        down = remote(
            oe.at[:, pl.ds(BLK, BLK)], oe.at[:, pl.ds(CELLS + BLK, BLK)],
            oh_ss.at[1], oh_rs.at[1], c, lax.rem(d + DOM - 1, DOM),
        )

        @pl.when(has_next)
        def _():
            up.start()

        @pl.when(has_prev)
        def _():
            down.start()

        st[...] = jnp.zeros((FIELDS * 2048, ELEMS), f32)
        zero_out = pltpu.make_async_copy(st, atm_hbm, zero_sem)
        zero_out.start()

        @pl.when(has_prev)
        def _():
            up.wait_recv()

        @pl.when(jnp.logical_not(has_prev))
        def _():
            oe[:, :BLK] = jnp.zeros((OROWS, BLK), f32)

        @pl.when(has_next)
        def _():
            down.wait_recv()

        @pl.when(jnp.logical_not(has_next))
        def _():
            oe[:, CELLS + BLK :] = jnp.zeros((OROWS, BLK), f32)

        source = iota((3 * BLK, BLK), 0)
        centre = source == iota((3 * BLK, BLK), 1) + BLK

        def cells(b, _):
            at = pl.multiple_of(b * BLK, BLK)
            here = pl.ds(at, BLK)
            rel = cell_nbr[:, here] - (d * CELLS + at - BLK)
            diff = cell_diff[:, here]
            total = jnp.sum(diff, axis=0, keepdims=True)
            mat = jnp.where(centre, jnp.broadcast_to(-total, (3 * BLK, BLK)), 0.0)
            for k in range(NBR_O):
                mat = mat + jnp.where(source == rel[k : k + 1, :], diff[k : k + 1, :], 0.0)
            lap = jnp.dot(
                oe[:, pl.ds(at, 3 * BLK)], mat, precision=highest, preferred_element_type=f32
            )
            for f in range(FIELDS):
                g = slice(f * OLEV, (f + 1) * OLEV)
                o = oe[g, pl.ds(at + BLK, BLK)]
                mix = jnp.dot(overt[...], o, precision=highest, preferred_element_type=f32)
                ob[g, here] = o + lap[g] + mix
            return 0

        lax.fori_loop(0, OBLOCKS, cells, 0)
        for comp in range(ATM):
            remote(ofl_s, ofl_r.at[comp], ofl_ss, ofl_rs.at[comp], comp, d).wait_recv()
        total = ofl_r[0] + ofl_r[1] + ofl_r[2]
        total = 0.5 * (total[:4] + total[4:])
        sea = mask[...] == 1
        first_row = iota((OLEV, CELLS), 0) == 0
        for f in range(FIELDS):
            g = slice(f * OLEV, (f + 1) * OLEV)
            fresh = ob[g, :] + jnp.where(first_row, total[f : f + 1, :], 0.0)
            ob[g, :] = jnp.where(sea, fresh, oe[g, BLK : BLK + CELLS])
        ocean_done = pltpu.make_async_copy(ob, ocean_out_hbm, out_sem.at[0])
        ocean_done.start()
        for copy in surf_out:
            copy.wait_send()

        @pl.when(has_next)
        def _():
            up.wait_send()

        @pl.when(has_prev)
        def _():
            down.wait_send()

        zero_out.wait()
        ocean_done.wait()


def local(
    atm_state, elem_nbr, elem_metric, bulk_coef, stiffness, coupling, atm_vertical,
    ocean_state, cell_nbr, cell_diff, ocean_vertical, sea_mask,
    pair_owner, pair_block, pair_src, remap_weight,
):
    vmem, sem = pltpu.VMEM, pltpu.SemaphoreType.DMA
    whole, anywhere = pl.BlockSpec(memory_space=pltpu.VMEM), pl.BlockSpec(memory_space=pl.ANY)
    big, halves = (BLOCKS, ROWS, LANES), (BLOCKS + 2, ROWS, LANES)
    message = (DOM, 8, BLK)
    scratch = [
        vmem((FIELDS * 2048, ELEMS), f32),
        vmem(big, f32), vmem(halves, bf16), vmem(halves, bf16),
        vmem(big, f32), vmem(halves, bf16), vmem(halves, bf16),
        vmem((2 * LEV, 2 * LEV), bf16), vmem((BLOCKS, 2 * LANES, LANES), bf16),
        vmem((BLOCKS, 2 * LANES, LANES), bf16), vmem((BLOCKS, 8, LANES), f32),
        vmem((5, NPTS, LANES), f32), vmem((BLOCKS, 8, 128), i32),
        vmem((BLOCKS, 8, LANES), f32), vmem((128, BLK), f32),
        vmem((PAIRS, BLK, BLK), f32), vmem((PAIRS, BLK, BLK), bf16), vmem((PAIRS, BLK, BLK), bf16),
        vmem((256, BLK), f32), vmem((256, BLK), f32),
        vmem((256, 256), bf16), vmem((256, 256), bf16), vmem((64, 256), bf16), vmem((256, 64), bf16),
        vmem((2, ROWS, 128), f32), vmem((2, ROWS, 128), f32),
        vmem((2, ROWS, 128), f32), vmem((2, ROWS, 128), f32),
        vmem(message, i32), vmem(message, i32), vmem(message, f32), vmem(message, f32),
        vmem(message, f32), vmem(message, f32),
        vmem((8, CELLS), f32), vmem((8, CELLS), f32), vmem((8, CELLS), f32),
        vmem((ATM, 8, CELLS), f32),
        vmem((OROWS, CELLS + 2 * BLK), f32), vmem((OROWS, CELLS), f32),
        sem((FIELDS,)), sem, sem, sem((FIELDS,)), sem,
        sem((DOM,)), sem((DOM,)), sem((DOM,)), sem((DOM,)), sem((DOM,)), sem((DOM,)),
        sem((ATM,)), sem, sem, sem((ATM,)),
        sem((2,)), sem((2,)), sem((2,)), sem((2,)), sem((2,)), sem((2,)),
    ]
    atm, ocean = pl.pallas_call(
        kernel,
        out_shape=(
            jax.ShapeDtypeStruct((FIELDS * 2048, ELEMS), f32),
            jax.ShapeDtypeStruct((OROWS, CELLS), f32),
        ),
        in_specs=[anywhere] * 3 + [whole] * 13,
        out_specs=(anywhere, anywhere),
        scratch_shapes=scratch,
        compiler_params=pltpu.CompilerParams(
            collective_id=0, has_side_effects=True, vmem_limit_bytes=60 << 20
        ),
        name="coupled_step",
    )(
        atm_state.reshape(FIELDS * 2048, ELEMS),
        remap_weight[0],
        ocean_state.reshape(OROWS, CELLS),
        elem_nbr[0], elem_metric[0], bulk_coef[0], stiffness, coupling, atm_vertical,
        cell_nbr[0], cell_diff[0], ocean_vertical, sea_mask,
        pair_owner[0], pair_block, pair_src,
    )
    return (
        atm.reshape(1, FIELDS, LEV, NPTS, ELEMS),
        ocean.reshape(1, FIELDS, OLEV, CELLS),
    )


def solution(mesh):
    in_specs = (
        P("comp", None, None, None, "dom"),
        P("comp", None, "dom"),
        P("comp", None, "dom"),
        P("comp", None, "dom"),
        P(),
        P(),
        P(),
        P("comp", None, None, "dom"),
        P("comp", None, "dom"),
        P("comp", None, "dom"),
        P(),
        P("comp", "dom"),
        P("comp", "dom", None),
        P("comp", "dom"),
        P("comp", "dom"),
        P("comp", "dom", None, None),
    )
    out_specs = (P("comp", None, None, None, "dom"), P("comp", None, None, "dom"))
    return jax.shard_map(local, mesh=mesh, in_specs=in_specs, out_specs=out_specs, check_vma=False)
```

profile of v0, /device:TPU:2, one launch (start us, length us, event | category | flops | bytes accessed | tf_op | source)
XLA Modules:
  0.0 52.6 jit_solution(10369921705491464641)
XLA Ops:
  0.6 1.3 %copy.18.owner = s32[32,1]{1,0:T(8,128)} copy(s32[32,1]{0,1:T(1,128)} %bitcast.25) | data formatting | bytes 256 | tf_op jit(solution)/shard_map/squeeze | solution.py:670
  2.0 1.4 %copy.24 = s32[1,6,1024]{2,1,0:T(8,128)} copy(s32[1,6,1024]{2,0,1:T(1,128)} %param.24) | data formatting | bytes 49152
  3.3 1.4 %copy.23 = f32[1,6,1024]{2,1,0:T(8,128)} copy(f32[1,6,1024]{2,0,1:T(1,128)} %param.25) | data formatting | bytes 49152
  4.7 42.2 %coupled_step.1 = (f32[8192,128]{1,0:T(8,128)}, f32[320,1024]{1,0:T(8,128)}) custom-call(f32[8192,128]{1,0:T(8,128)} %bitcast.15, f32[32,128,128]{2,1,0:T(8,128)} %bitcast.17, f32[320,1024]{1,0:T(8,128)} %bitcast.19, s32[4,128]{1,0:T(4,128)} %bitcast.24, f32[16,128]{1,0:T(8,128)} %bitcast.22, f32[16,128]{1,0:T(8,128)} %bitcast.23, f32[16,16]{1,0:T(8,128)} %stiff.1, ...), custom_call_target="tpu_custom_call" | custom-call | tf_op jit(solution)/shard_map/coupled_step/pallas_call | solution.py:651
  46.8 0.0 copy-start
  46.9 4.7 %copy.27 = f32[1,4,128,16,128]{4,3,2,1,0:T(8,128)} copy(f32[1,4,128,16,128]{4,3,2,1,0:T(8,128)} %bitcast.16) | data formatting | bytes 8388608
  51.5 0.0 copy-done
  51.5 1.1 %copy.28 = f32[1,4,80,1024]{3,2,1,0:T(8,128)} copy(f32[1,4,80,1024]{3,2,1,0:T(8,128)S(1)} %bitcast.18) | data formatting | bytes 2621440
Async XLA Ops:
  46.8 4.7 %copy-start = (f32[320,1024]{1,0:T(8,128)S(1)}, f32[320,1024]{1,0:T(8,128)}, u32[]{:S(2)}) copy-start(f32[320,1024]{1,0:T(8,128)} %get-tuple-element.5) | copy-start | bytes 3932164
where the time goes:
time: 52.9 us; the launch traced here: 52.6 us
  Pallas kernels  42.2 us (80%)
  local copies, waits for them, and re-layouts  9.79 us (19%)
  between operations  0.65 us (1%)
    pallas_call x1, Pallas kernels, local(): pl.pallas_call(kernel, out_shape=(jax.ShapeDtypeStruct((FIELDS * 2048, EL...  42.2 us
    unnamed x6, local copies, waits for them, and re-layouts  8.45 us
    squeeze x1, local copies, waits for them, and re-layouts, local(): pair_owner[0]  1.34 us

commit v1 on v0

--- a/solution.py
+++ b/solution.py
@@ -26,14 +26,21 @@
     return lax.broadcasted_iota(i32, shape, axis)
 
 
-def swap_chunks(a):
+def exchange_chunks(a):
     chunk = iota(a[0].shape, 1) // WIDTH
-    a = [a[q] if q == 0 else pltpu.roll(a[q], WIDTH * q, 1) for q in range(8)]
     for k in (1, 2, 4):
         take = (chunk & k) != 0
         a = [jnp.where(take, a[(i + k) % 8], a[i]) for i in range(8)]
-    out = [a[(-b) % 8] for b in range(8)]
-    return [out[b] if b == 0 else pltpu.roll(out[b], 128 - WIDTH * b, 1) for b in range(8)]
+    return [a[(-b) % 8] for b in range(8)]
+
+
+def to_blocks(a):
+    return exchange_chunks([a[q] if q == 0 else pltpu.roll(a[q], WIDTH * q, 1) for q in range(8)])
+
+
+def from_blocks(a):
+    a = exchange_chunks(a)
+    return [a[q] if q == 0 else pltpu.roll(a[q], 128 - WIDTH * q, 1) for q in range(8)]
 
 
 def split(x):
@@ -53,7 +60,7 @@
         row = f * LEV + i * 16
         for h in range(2):
             a = [st[pl.ds(row * NPTS + h * 8 + q, 16, stride=NPTS), :] for q in range(8)]
-            w = swap_chunks(a)
+            w = to_blocks(a)
             cols = slice(h * 128, (h + 1) * 128)
             for b in range(BLOCKS):
                 hi, lo = split(w[b])
@@ -70,7 +77,7 @@
         row = f * LEV + i * 16
         for h in range(2):
             cols = slice(h * 128, (h + 1) * 128)
-            w = swap_chunks([x[b, pl.ds(row, 16), cols] for b in range(BLOCKS)])
+            w = from_blocks([x[b, pl.ds(row, 16), cols] for b in range(BLOCKS)])
             for q in range(8):
                 st[pl.ds(row * NPTS + h * 8 + q, 16, stride=NPTS), :] = w[q]
         return 0
@@ -86,13 +93,13 @@
             mat, spread, (((0,), (0,)), ((), ())), precision=highest, preferred_element_type=f32
         )
     for h in range(2):
-        w = swap_chunks(
+        w = to_blocks(
             [jnp.broadcast_to(metric[h * 8 + q : h * 8 + q + 1, :], (8, 128)) for q in range(8)]
         )
         for b in range(BLOCKS):
             met[b, :, h * 128 : (h + 1) * 128] = w[b]
     own = jnp.concatenate([nbr[...], nbr[...]], axis=0) - first
-    w = swap_chunks([own] * 8)
+    w = to_blocks([own] * 8)
     for b in range(BLOCKS):
         near[b] = w[b] - b * WIDTH
     hi, lo = split(vert[...])
@@ -102,8 +109,12 @@
     vv[LEV:, LEV:] = jnp.zeros((LEV, LEV), bf16)
 
 
-def operator_block(b, near, cr, th, tl):
+def operator_block(b, near, cr, turned, th, tl):
     sub, lane = iota((WIDTH, LANES), 0), iota((WIDTH, LANES), 1)
+    for s in range(5):
+        for h in range(2):
+            cols = slice(h * 128, (h + 1) * 128)
+            turned[s, :, cols] = pltpu.roll(cr[s, :, cols], b * WIDTH, 1)
     rows = near[b]
     inner, outer = [], []
     for s in range(4):
@@ -114,16 +125,25 @@
         inner.append(hit & inside)
         outer.append(hit & jnp.logical_not(inside))
     diag = sub == (lane & (WIDTH - 1))
-    for q in range(NPTS):
-        vals = [jnp.broadcast_to(cr[s, q : q + 1, :], (WIDTH, LANES)) for s in range(5)]
-        c = jnp.where(diag, vals[4], 0.0)
+    half = (WIDTH // 2, LANES)
+
+    def row(s, q, shape):
+        return jnp.broadcast_to(turned[s, pl.ds(q, 1), :], shape)
+
+    for k in range(NPTS):
+        h, chunk = k - k % 8, k % 8
+        q = h + ((chunk - b + 8) & 7)
+        after = h + ((chunk - b + 7) & 7)
+        before = h + ((chunk - b + 9) & 7)
+        c = jnp.where(diag, row(4, q, (WIDTH, LANES)), 0.0)
         d = jnp.zeros((WIDTH, LANES), f32)
         for s in range(4):
-            c = c + jnp.where(inner[s], vals[s], 0.0)
-            d = d + jnp.where(outer[s], vals[s], 0.0)
+            c = c + jnp.where(inner[s], row(s, q, (WIDTH, LANES)), 0.0)
+            sides = jnp.concatenate([row(s, after, half), row(s, before, half)], axis=0)
+            d = d + jnp.where(outer[s], sides, 0.0)
         for base, part in ((0, c), (LANES, d)):
             hi, lo = split(part)
-            here = slice(base + q * WIDTH, base + (q + 1) * WIDTH)
+            here = slice(base + k * WIDTH, base + (k + 1) * WIDTH)
             th[b, here, :] = hi
             tl[b, here, :] = lo
 
@@ -148,31 +168,28 @@
             yl[b + 1, g] = lo
 
 
-def add_surface(delta, y, yh, yl):
+def add_surface(b, delta, y, yh, yl):
     last = iota((16, LANES), 0) == 15
-
-    def body(b, _):
-        for f in range(FIELDS):
-            g = slice((f + 1) * LEV - 16, (f + 1) * LEV)
-            new = y[b, g] + jnp.where(
-                last, jnp.broadcast_to(delta[b, f : f + 1, :], (16, LANES)), 0.0
-            )
-            y[b, g] = new
-            if yh is not None:
-                hi, lo = split(new)
-                yh[b + 1, g] = hi
-                yl[b + 1, g] = lo
-        return 0
-
-    lax.fori_loop(0, BLOCKS, body, 0)
-
-
-def edges_out(x, es):
-    low = (iota((ROWS, 128), 1) & (WIDTH - 1)) < WIDTH // 2
-    top = x[BLOCKS - 1]
-    es[0] = jnp.where(low, pltpu.roll(top[:, 128:], 120, 1), top[:, :128])
-    bottom = x[0]
-    es[1] = jnp.where(low, bottom[:, :128], pltpu.roll(bottom[:, 128:], 8, 1))
+    for f in range(FIELDS):
+        g = slice((f + 1) * LEV - 16, (f + 1) * LEV)
+        new = y[b, g] + jnp.where(last, jnp.broadcast_to(delta[b, f : f + 1, :], (16, LANES)), 0.0)
+        y[b, g] = new
+        if yh is not None:
+            hi, lo = split(new)
+            yh[b + 1, g] = hi
+            yl[b + 1, g] = lo
+
+
+def fold_edges(top, bottom):
+    low = (iota((top.shape[0], 128), 1) & (WIDTH - 1)) < WIDTH // 2
+    up = jnp.where(low, pltpu.roll(top[:, 128:], 120, 1), top[:, :128])
+    down = jnp.where(low, bottom[:, :128], pltpu.roll(bottom[:, 128:], 8, 1))
+    return up, down
+
+
+def edges_out(f, x, es):
+    g = slice(f * LEV, (f + 1) * LEV)
+    es[0, g], es[1, g] = fold_edges(x[BLOCKS - 1, g], x[0, g])
 
 
 def edges_in(er, xh, xl):
@@ -196,7 +213,7 @@
         wide = jnp.broadcast_to(row.astype(f32), (PAIRS, PAIRS))
         return jnp.sum(jnp.where(eye, wide, 0.0), axis=1, keepdims=True)
 
-    own = jnp.broadcast_to(owner[...].astype(f32), (PAIRS, 256))
+    own = jnp.broadcast_to(as_column(owner[...]), (PAIRS, 256))
     own_c = over_columns(own)
     rank_c = jnp.sum(jnp.where((own == own_c) & (pair < col), 1.0, 0.0), axis=0, keepdims=True)
     slot_c = 2.0 * own_c + rank_c
@@ -220,8 +237,8 @@
     dims = (((1,), (1 if transposed else 0,)), ((), ()))
 
     def body(i, _):
-        for k in range(8):
-            j = i * 8 + k
+        for k in range(16):
+            j = i * 16 + k
             v = rows[pl.ds(j * 8, 8), :]
             both = jnp.concatenate([v, v - v.astype(bf16).astype(f32)], axis=0).astype(bf16)
             a = lax.dot_general(both, wh[j], dims, preferred_element_type=f32)
@@ -229,22 +246,25 @@
             out[pl.ds(j * 8, 8), :] = a[:8] + a[8:] + b[:8]
         return 0
 
-    lax.fori_loop(0, PAIRS // 8, body, 0)
+    lax.fori_loop(0, PAIRS // 16, body, 0)
 
 
 def kernel(
-    state_hbm, weight_hbm, ocean_hbm, nbr, metric, coef, stiff, coup, vert,
-    cell_nbr, cell_diff, overt, mask, owner, block, src,
-    atm_hbm, ocean_out_hbm,
-    st, x, xh, xl, y, yh, yl, vv, th, tl, met, cr, near, delta, flux,
+    state_hbm, weight_hbm, ocean_hbm,
+    nbr_h, metric_h, coef_h, stiff_h, coup_h, vert_h, owner_h, block_h, src_h,
+    cell_nbr_h, cell_diff_h, overt_h, mask_h,
+    packed_hbm, ocean_out_hbm,
+    nbr, metric, coef, stiff, coup, vert, owner, block, src,
+    cell_nbr, cell_diff, overt, mask,
+    st, x, xh, xl, y, yh, yl, vv, th, tl, met, cr, turned, near, delta, flux,
     wt, wh, wl, rows_a, rows_b, slot_of, slot_to, point_of, point_to,
-    es, er, es2, er2,
+    es, er, es2, er2, es3, er3,
     ids_s, ids_r, rep_s, rep_r, flx_s, flx_r, surf_s, surf_r, ofl_s, ofl_r,
     oe, ob,
-    st_sem, wt_sem, oc_sem, out_sem, zero_sem,
+    small_sem, st_sem, wt_sem, oc_sem, out_sem,
     ids_ss, ids_rs, rep_ss, rep_rs, flx_ss, flx_rs,
     surf_ss, surf_rs, ofl_ss, ofl_rs,
-    edge_ss, edge_rs, edge2_ss, edge2_rs, oh_ss, oh_rs,
+    edge_ss, edge_rs, edge2_ss, edge2_rs, edge3_ss, edge3_rs, oh_ss, oh_rs,
 ):
     c, d = lax.axis_index("comp"), lax.axis_index("dom")
     barrier = pltpu.get_barrier_semaphore()
@@ -259,46 +279,55 @@
     def greet(comp, dom):
         pl.semaphore_signal(barrier, inc=1, device_id=(comp, dom), device_id_type=MESH)
 
+    def fetch(pairs, first):
+        copies = [
+            pltpu.make_async_copy(a, b, small_sem.at[first + i]) for i, (a, b) in enumerate(pairs)
+        ]
+        for copy in copies:
+            copy.start()
+        return copies
+
     @pl.when(c < ATM)
     def _atmosphere():
+        has_prev, has_next = (c + d) > 0, (c * DOM + d) < ATM * DOM - 1
+        prev_c, prev_d = jnp.where(d == 0, c - 1, c), lax.rem(d + DOM - 1, DOM)
+        next_c, next_d = jnp.where(d == DOM - 1, c + 1, c), lax.rem(d + 1, DOM)
+        cross_prev = (d == 0) & (c > 0)
+        cross_next = (d == DOM - 1) & (c < ATM - 1)
+
+        def other(i):
+            return lax.rem(d + i, DOM)
+
+        def hello(i, _):
+            greet(c, other(i))
+            return 0
+
         state_in = [
             pltpu.make_async_copy(
                 state_hbm.at[pl.ds(f * 2048, 2048)], st.at[pl.ds(f * 2048, 2048)], st_sem.at[f]
             )
             for f in range(FIELDS)
         ]
-        for copy in state_in:
+        state_in[0].start()
+        lax.fori_loop(1, DOM, hello, 0)
+        greet(ocean_slab, d)
+
+        @pl.when(cross_prev)
+        def _():
+            greet(prev_c, prev_d)
+
+        @pl.when(cross_next)
+        def _():
+            greet(next_c, next_d)
+
+        for copy in state_in[1:]:
             copy.start()
+        small_in = fetch(
+            [(owner_h, owner), (block_h, block), (src_h, src), (nbr_h, nbr), (metric_h, metric),
+             (coef_h, coef), (stiff_h, stiff), (coup_h, coup), (vert_h, vert)], 0,
+        )
         weights_in = pltpu.make_async_copy(weight_hbm, wt, wt_sem)
         weights_in.start()
-        has_prev, has_next = (c + d) > 0, (c * DOM + d) < ATM * DOM - 1
-        prev_c, prev_d = jnp.where(d == 0, c - 1, c), lax.rem(d + DOM - 1, DOM)
-        next_c, next_d = jnp.where(d == DOM - 1, c + 1, c), lax.rem(d + 1, DOM)
-
-        def other(i):
-            return lax.rem(d + i, DOM)
-
-        def hello(i, _):
-            greet(c, other(i))
-            return 0
-
-        lax.fori_loop(1, DOM, hello, 0)
-        greet(ocean_slab, d)
-        cross_prev = (d == 0) & (c > 0)
-        cross_next = (d == DOM - 1) & (c < ATM - 1)
-
-        @pl.when(cross_prev)
-        def _():
-            greet(prev_c, prev_d)
-
-        @pl.when(cross_next)
-        def _():
-            greet(next_c, next_d)
-
-        pair_tables(owner, block, src, slot_of, slot_to, point_of, point_to, ids_s)
-        pl.semaphore_wait(
-            barrier, DOM + jnp.where(cross_prev, 1, 0) + jnp.where(cross_next, 1, 0)
-        )
 
         def exchange(out, into, send, recv):
             def copy(i):
@@ -333,11 +362,10 @@
         ids_start, ids_arrive, ids_sent = exchange(ids_s, ids_r, ids_ss, ids_rs)
         rep_start, rep_arrive, rep_sent = exchange(rep_s, rep_r, rep_ss, rep_rs)
         flx_start, flx_arrive, flx_sent = exchange(flx_s, flx_r, flx_ss, flx_rs)
-        ids_start()
-
-        def edge_copies(out, into, send, recv):
-            up = remote(out.at[0], into.at[0], send.at[0], recv.at[0], next_c, next_d)
-            down = remote(out.at[1], into.at[1], send.at[1], recv.at[1], prev_c, prev_d)
+
+        def edge_copies(out, into, send, recv, rows):
+            up = remote(out.at[0, rows], into.at[0, rows], send.at[0], recv.at[0], next_c, next_d)
+            down = remote(out.at[1, rows], into.at[1, rows], send.at[1], recv.at[1], prev_c, prev_d)
 
             def start():
                 @pl.when(has_next)
@@ -348,14 +376,6 @@
                 def _():
                     down.start()
 
-                @pl.when(jnp.logical_not(has_prev))
-                def _():
-                    into[0] = jnp.zeros((ROWS, 128), f32)
-
-                @pl.when(jnp.logical_not(has_next))
-                def _():
-                    into[1] = jnp.zeros((ROWS, 128), f32)
-
             def arrive():
                 @pl.when(has_prev)
                 def _():
@@ -376,19 +396,50 @@
 
             return start, arrive, sent
 
-        edge_start, edge_arrive, edge_sent = edge_copies(es, er, edge_ss, edge_rs)
-        edge2_start, edge2_arrive, edge2_sent = edge_copies(es2, er2, edge2_ss, edge2_rs)
-
-        for f in range(FIELDS):
+        edges = [
+            edge_copies(es, er, edge_ss.at[f], edge_rs.at[f], pl.ds(f * LEV, LEV))
+            for f in range(FIELDS)
+        ]
+        edge2_start, edge2_arrive, edge2_sent = edge_copies(
+            es2, er2, edge2_ss, edge2_rs, pl.ds(0, ROWS)
+        )
+        edge3_start, edge3_arrive, edge3_sent = edge_copies(
+            es3, er3, edge3_ss, edge3_rs, pl.ds(0, 8)
+        )
+
+        @pl.when(jnp.logical_not(has_prev))
+        def _():
+            er[0] = jnp.zeros((ROWS, 128), f32)
+            er2[0] = jnp.zeros((ROWS, 128), f32)
+            er3[0] = jnp.zeros((8, 128), f32)
+
+        @pl.when(jnp.logical_not(has_next))
+        def _():
+            er[1] = jnp.zeros((ROWS, 128), f32)
+            er2[1] = jnp.zeros((ROWS, 128), f32)
+            er3[1] = jnp.zeros((8, 128), f32)
+
+        state_in[0].wait()
+        pack(0, st, x, xh, xl)
+        edges_out(0, x, es)
+        for copy in small_in:
+            copy.wait()
+        pair_tables(owner, block, src, slot_of, slot_to, point_of, point_to, ids_s)
+        pl.semaphore_wait(
+            barrier, DOM + jnp.where(cross_prev, 1, 0) + jnp.where(cross_next, 1, 0)
+        )
+        edges[0][0]()
+        ids_start()
+        for f in range(1, FIELDS):
             state_in[f].wait()
             pack(f, st, x, xh, xl)
-        edges_out(x, es)
-        edge_start()
+            edges_out(f, x, es)
+            edges[f][0]()
 
         small_tables(c * (DOM * ELEMS) + d * ELEMS, nbr, metric, stiff, coup, vert, cr, met, near, vv)
 
         def table(b, _):
-            operator_block(b, near, cr, th, tl)
+            operator_block(b, near, cr, turned, th, tl)
             return 0
 
         lax.fori_loop(0, BLOCKS, table, 0)
@@ -418,12 +469,20 @@
         lax.fori_loop(0, PAIRS, halves, 0, unroll=2)
 
         def first(i, _):
-            @pl.when(i == BLOCKS - 2)
+            @pl.when(i == 4)
             def _():
-                edge_arrive()
+                for f in range(FIELDS):
+                    edges[f][1]()
                 edges_in(er, xh, xl)
 
-            b = jnp.where(i < BLOCKS - 2, i + 1, (i - (BLOCKS - 2)) * (BLOCKS - 1))
+            @pl.when(i == 6)
+            def _():
+                for f in range(FIELDS):
+                    edges_out(f, y, es2)
+                edge2_start()
+
+            edge = jnp.where(i == 4, 0, BLOCKS - 1)
+            b = jnp.where(i < 4, i + 1, jnp.where(i < 6, edge, i - 1))
             advance(b, x, xh, xl, y, yh, yl, vv, th, tl, met)
             return 0
 
@@ -445,18 +504,24 @@
         flux[:64] = fl * -0.5
         flux[64:] = jnp.zeros((64, BLK), f32)
         for h in range(2):
-            w = swap_chunks([flux[pl.ds(h * 8 + q, 8, stride=NPTS), :] for q in range(8)])
+            w = to_blocks([flux[pl.ds(h * 8 + q, 8, stride=NPTS), :] for q in range(8)])
             for b in range(BLOCKS):
                 delta[b, :, h * 128 : (h + 1) * 128] = w[b]
-        add_surface(delta, y, yh, yl)
-        edges_out(y, es2)
-        edge2_start()
+        es3[0], es3[1] = fold_edges(delta[BLOCKS - 1], delta[0])
+        edge3_start()
+
+        def surface_term(b, _):
+            add_surface(b, delta, y, yh, yl)
+            return 0
+
+        lax.fori_loop(0, BLOCKS, surface_term, 0)
+
+        def block_out(b):
+            return pltpu.make_async_copy(x.at[b], packed_hbm.at[b], out_sem.at[b])
 
         def second(i, _):
-            @pl.when(i == BLOCKS - 2)
+            @pl.when(i == 3)
             def _():
-                edge2_arrive()
-                edges_in(er2, yh, yl)
                 flx_arrive()
 
                 def gather(j, accs):
@@ -471,40 +536,44 @@
                     ofl_s[:, b * BLK : (b + 1) * BLK] = accs[b]
                 remote(ofl_s, ofl_r.at[c], ofl_ss, ofl_rs.at[c], ocean_slab, d).start()
 
+            @pl.when(i == BLOCKS - 2)
+            def _():
+                edge2_arrive()
+                edge3_arrive()
+                last = iota((16, 128), 0) == 15
+                for side in range(2):
+                    for f in range(FIELDS):
+                        g = slice((f + 1) * LEV - 16, (f + 1) * LEV)
+                        extra = jnp.broadcast_to(er3[side, f : f + 1, :], (16, 128))
+                        er2[side, g] = er2[side, g] + jnp.where(last, extra, 0.0)
+                edges_in(er2, yh, yl)
+
             b = jnp.where(i < BLOCKS - 2, i + 1, (i - (BLOCKS - 2)) * (BLOCKS - 1))
             advance(b, y, yh, yl, x, None, None, vv, th, tl, met)
+            add_surface(b, delta, x, None, None)
+            block_out(b).start()
             return 0
 
         lax.fori_loop(0, BLOCKS, second, 0)
-        add_surface(delta, x, None, None)
-
-        ob[...] = jnp.zeros((OROWS, CELLS), f32)
-        zero_out = pltpu.make_async_copy(ob, ocean_out_hbm, zero_sem)
-        zero_out.start()
-        outs = [
-            pltpu.make_async_copy(
-                st.at[pl.ds(f * 2048, 2048)], atm_hbm.at[pl.ds(f * 2048, 2048)], out_sem.at[f]
-            )
-            for f in range(FIELDS)
-        ]
-        for f in range(FIELDS):
-            unpack(f, x, st)
-            outs[f].start()
         ids_sent()
         rep_sent()
         flx_sent()
-        edge_sent()
+        for f in range(FIELDS):
+            edges[f][2]()
         edge2_sent()
+        edge3_sent()
         remote(ofl_s, ofl_r.at[c], ofl_ss, ofl_rs.at[c], ocean_slab, d).wait_send()
-        zero_out.wait()
-        for copy in outs:
-            copy.wait()
+        for b in range(BLOCKS):
+            block_out(b).wait()
 
     @pl.when(c == ocean_slab)
     def _ocean():
         mid = oe.at[:, pl.ds(BLK, CELLS)]
         ocean_in = pltpu.make_async_copy(ocean_hbm, mid, oc_sem)
         ocean_in.start()
+        small_in = fetch(
+            [(cell_nbr_h, cell_nbr), (cell_diff_h, cell_diff), (overt_h, overt), (mask_h, mask)], 0
+        )
         for comp in range(ATM):
             greet(comp, d)
         has_prev, has_next = d > 0, d < DOM - 1
@@ -546,10 +615,6 @@
         def _():
             down.start()
 
-        st[...] = jnp.zeros((FIELDS * 2048, ELEMS), f32)
-        zero_out = pltpu.make_async_copy(st, atm_hbm, zero_sem)
-        zero_out.start()
-
         @pl.when(has_prev)
         def _():
             up.wait_recv()
@@ -566,18 +631,19 @@
         def _():
             oe[:, CELLS + BLK :] = jnp.zeros((OROWS, BLK), f32)
 
+        for copy in small_in:
+            copy.wait()
         source = iota((3 * BLK, BLK), 0)
         centre = source == iota((3 * BLK, BLK), 1) + BLK
 
         def cells(b, _):
             at = pl.multiple_of(b * BLK, BLK)
             here = pl.ds(at, BLK)
-            rel = cell_nbr[:, here] - (d * CELLS + at - BLK)
-            diff = cell_diff[:, here]
-            total = jnp.sum(diff, axis=0, keepdims=True)
-            mat = jnp.where(centre, jnp.broadcast_to(-total, (3 * BLK, BLK)), 0.0)
+            rel = [cell_nbr[k, :, here] - (d * CELLS + at - BLK) for k in range(NBR_O)]
+            diff = [cell_diff[k, :, here] for k in range(NBR_O)]
+            mat = jnp.where(centre, jnp.broadcast_to(-sum(diff), (3 * BLK, BLK)), 0.0)
             for k in range(NBR_O):
-                mat = mat + jnp.where(source == rel[k : k + 1, :], diff[k : k + 1, :], 0.0)
+                mat = mat + jnp.where(source == rel[k], diff[k], 0.0)
             lap = jnp.dot(
                 oe[:, pl.ds(at, 3 * BLK)], mat, precision=highest, preferred_element_type=f32
             )
@@ -612,8 +678,49 @@
         def _():
             down.wait_send()
 
+        ocean_done.wait()
+
+
+def finish(packed_hbm, ocean_hbm, atm_hbm, ocean_out_hbm, x, st, blank, in_sem, out_sem, oc_sem):
+    c = lax.axis_index("comp")
+    outs = [
+        pltpu.make_async_copy(
+            st.at[pl.ds(f * 2048, 2048)], atm_hbm.at[pl.ds(f * 2048, 2048)], out_sem.at[f]
+        )
+        for f in range(FIELDS)
+    ]
+
+    @pl.when(c < ATM)
+    def _():
+        ins = [
+            pltpu.make_async_copy(
+                packed_hbm.at[:, pl.ds(f * LEV, LEV)], x.at[:, pl.ds(f * LEV, LEV)], in_sem.at[f]
+            )
+            for f in range(FIELDS)
+        ]
+        for copy in ins:
+            copy.start()
+        blank[...] = jnp.zeros((OROWS, CELLS), f32)
+        zero_out = pltpu.make_async_copy(blank, ocean_out_hbm, oc_sem)
+        zero_out.start()
+        for f in range(FIELDS):
+            ins[f].wait()
+            unpack(f, x, st)
+            outs[f].start()
         zero_out.wait()
-        ocean_done.wait()
+        for copy in outs:
+            copy.wait()
+
+    @pl.when(c == ATM)
+    def _():
+        ocean_out = pltpu.make_async_copy(ocean_hbm, ocean_out_hbm, oc_sem)
+        ocean_out.start()
+        for f in range(FIELDS):
+            st[f * 2048 : (f + 1) * 2048] = jnp.zeros((2048, ELEMS), f32)
+            outs[f].start()
+        ocean_out.wait()
+        for copy in outs:
+            copy.wait()
 
 
 def local(
@@ -622,39 +729,43 @@
     pair_owner, pair_block, pair_src, remap_weight,
 ):
     vmem, sem = pltpu.VMEM, pltpu.SemaphoreType.DMA
-    whole, anywhere = pl.BlockSpec(memory_space=pltpu.VMEM), pl.BlockSpec(memory_space=pl.ANY)
+    anywhere = pl.BlockSpec(memory_space=pl.ANY)
     big, halves = (BLOCKS, ROWS, LANES), (BLOCKS + 2, ROWS, LANES)
     message = (DOM, 8, BLK)
     scratch = [
+        vmem((4, ELEMS), i32), vmem((NPTS, ELEMS), f32), vmem((NPTS, ELEMS), f32),
+        vmem((NPTS, NPTS), f32), vmem((4, NPTS, NPTS), f32), vmem((LEV, LEV), f32),
+        vmem((1, PAIRS), i32), vmem((1, PAIRS), i32), vmem((1, PAIRS), i32),
+        vmem((NBR_O, 1, CELLS), i32), vmem((NBR_O, 1, CELLS), f32), vmem((OLEV, OLEV), f32),
+        vmem((1, CELLS), i32),
         vmem((FIELDS * 2048, ELEMS), f32),
         vmem(big, f32), vmem(halves, bf16), vmem(halves, bf16),
         vmem(big, f32), vmem(halves, bf16), vmem(halves, bf16),
         vmem((2 * LEV, 2 * LEV), bf16), vmem((BLOCKS, 2 * LANES, LANES), bf16),
         vmem((BLOCKS, 2 * LANES, LANES), bf16), vmem((BLOCKS, 8, LANES), f32),
-        vmem((5, NPTS, LANES), f32), vmem((BLOCKS, 8, 128), i32),
+        vmem((5, NPTS, LANES), f32), vmem((5, NPTS, LANES), f32), vmem((BLOCKS, 8, 128), i32),
         vmem((BLOCKS, 8, LANES), f32), vmem((128, BLK), f32),
         vmem((PAIRS, BLK, BLK), f32), vmem((PAIRS, BLK, BLK), bf16), vmem((PAIRS, BLK, BLK), bf16),
         vmem((256, BLK), f32), vmem((256, BLK), f32),
         vmem((256, 256), bf16), vmem((256, 256), bf16), vmem((64, 256), bf16), vmem((256, 64), bf16),
         vmem((2, ROWS, 128), f32), vmem((2, ROWS, 128), f32),
         vmem((2, ROWS, 128), f32), vmem((2, ROWS, 128), f32),
+        vmem((2, 8, 128), f32), vmem((2, 8, 128), f32),
         vmem(message, i32), vmem(message, i32), vmem(message, f32), vmem(message, f32),
         vmem(message, f32), vmem(message, f32),
         vmem((8, CELLS), f32), vmem((8, CELLS), f32), vmem((8, CELLS), f32),
         vmem((ATM, 8, CELLS), f32),
         vmem((OROWS, CELLS + 2 * BLK), f32), vmem((OROWS, CELLS), f32),
-        sem((FIELDS,)), sem, sem, sem((FIELDS,)), sem,
+        sem((9,)), sem((FIELDS,)), sem, sem, sem((BLOCKS,)),
         sem((DOM,)), sem((DOM,)), sem((DOM,)), sem((DOM,)), sem((DOM,)), sem((DOM,)),
         sem((ATM,)), sem, sem, sem((ATM,)),
-        sem((2,)), sem((2,)), sem((2,)), sem((2,)), sem((2,)), sem((2,)),
+        sem((FIELDS, 2)), sem((FIELDS, 2)), sem((2,)), sem((2,)), sem((2,)), sem((2,)),
+        sem((2,)), sem((2,)),
     ]
-    atm, ocean = pl.pallas_call(
+    packed, ocean = pl.pallas_call(
         kernel,
-        out_shape=(
-            jax.ShapeDtypeStruct((FIELDS * 2048, ELEMS), f32),
-            jax.ShapeDtypeStruct((OROWS, CELLS), f32),
-        ),
-        in_specs=[anywhere] * 3 + [whole] * 13,
+        out_shape=(jax.ShapeDtypeStruct(big, f32), jax.ShapeDtypeStruct((OROWS, CELLS), f32)),
+        in_specs=[anywhere] * 16,
         out_specs=(anywhere, anywhere),
         scratch_shapes=scratch,
         compiler_params=pltpu.CompilerParams(
@@ -666,9 +777,25 @@
         remap_weight[0],
         ocean_state.reshape(OROWS, CELLS),
         elem_nbr[0], elem_metric[0], bulk_coef[0], stiffness, coupling, atm_vertical,
-        cell_nbr[0], cell_diff[0], ocean_vertical, sea_mask,
-        pair_owner[0], pair_block, pair_src,
+        pair_owner.reshape(1, PAIRS), pair_block, pair_src,
+        jnp.transpose(cell_nbr, (1, 0, 2)), jnp.transpose(cell_diff, (1, 0, 2)),
+        ocean_vertical, sea_mask,
     )
+    atm, ocean = pl.pallas_call(
+        finish,
+        out_shape=(
+            jax.ShapeDtypeStruct((FIELDS * 2048, ELEMS), f32),
+            jax.ShapeDtypeStruct((OROWS, CELLS), f32),
+        ),
+        in_specs=[anywhere] * 2,
+        out_specs=(anywhere, anywhere),
+        scratch_shapes=[
+            vmem(big, f32), vmem((FIELDS * 2048, ELEMS), f32), vmem((OROWS, CELLS), f32),
+            sem((FIELDS,)), sem((FIELDS,)), sem,
+        ],
+        compiler_params=pltpu.CompilerParams(vmem_limit_bytes=60 << 20),
+        name="finish",
+    )(packed, ocean)
     return (
         atm.reshape(1, FIELDS, LEV, NPTS, ELEMS),
         ocean.reshape(1, FIELDS, OLEV, CELLS),

time: 52.9 us -> 76.9 us (1.45)
  the two profiles are of different devices: /device:TPU:2 before, /device:TPU:6 now
where the time goes in v1:
time: 76.9 us; the launch traced here: 76.8 us
  Pallas kernels  76.2 us (99%)
    pallas_call x1, Pallas kernels, local(): pl.pallas_call(finish, out_shape=(jax.ShapeDtypeStruct((FIELDS * 2048, EL...  40.9 us
    pallas_call x1, Pallas kernels, local(): pl.pallas_call(kernel, out_shape=(jax.ShapeDtypeStruct(big, f32), jax.Sha...  35.3 us

profile of v1, /device:TPU:6, one launch (start us, length us, event | category | flops | bytes accessed | tf_op | source)
XLA Modules:
  0.0 76.8 jit_solution(17448295441650933528)
XLA Ops:
  0.6 35.3 %coupled_step.1 = (f32[8,512,256]{2,1,0:T(8,128)}, f32[320,1024]{1,0:T(8,128)}) custom-call(f32[8192,128]{1,0:T(8,128)} %bitcast.11, f32[32,128,128]{2,1,0:T(8,128)} %bitcast.12, f32[320,1024]{1,0:T(8,128)} %bitcast.13, s32[4,128]{1,0:T(4,128)} %bitcast.18, f32[16,128]{1,0:T(8,128)} %bitcast.16, f32[16,128]{1,0:T(8,128)} %bitcast.17, f32[16,16]{1,0:T(8,128)} %stiff_h.1, ...), custom_call_target="tpu_custom_call" | custom-call | tf_op jit(solution)/shard_map/coupled_step/pallas_call | solution.py:765
  35.9 40.9 %finish.1 = (f32[8192,128]{1,0:T(8,128)}, f32[320,1024]{1,0:T(8,128)}) custom-call(f32[8,512,256]{2,1,0:T(8,128)} %get-tuple-element.6.packed_hbm, f32[320,1024]{1,0:T(8,128)} %get-tuple-element.7.ocean_hbm), custom_call_target="tpu_custom_call" | custom-call | tf_op jit(solution)/shard_map/finish/pallas_call | solution.py:784

commit v2 on v1

--- a/solution.py
+++ b/solution.py
@@ -72,9 +72,9 @@
     lax.fori_loop(0, LEV // 16, body, 0, unroll=2)
 
 
-def unpack(f, x, st):
+def unpack(first, levels, x, st):
     def body(i, _):
-        row = f * LEV + i * 16
+        row = first + i * 16
         for h in range(2):
             cols = slice(h * 128, (h + 1) * 128)
             w = from_blocks([x[b, pl.ds(row, 16), cols] for b in range(BLOCKS)])
@@ -82,7 +82,7 @@
                 st[pl.ds(row * NPTS + h * 8 + q, 16, stride=NPTS), :] = w[q]
         return 0
 
-    lax.fori_loop(0, LEV // 16, body, 0, unroll=2)
+    lax.fori_loop(0, levels // 16, body, 0, unroll=2)
 
 
 def small_tables(first, nbr, metric, stiff, coup, vert, cr, met, near, vv):
@@ -148,7 +148,8 @@
             tl[b, here, :] = lo
 
 
-def advance(b, x, xh, xl, y, yh, yl, vv, th, tl, met):
+def advance(b, x, xh, xl, y, yh, yl, vv, th, tl, met, delta=None):
+    last = iota((16, LANES), 0) == 15
     low = (iota((ROWS, LANES), 1) & (WIDTH - 1)) < WIDTH // 2
     sh = jnp.where(low, xh[b + 2], xh[b])
     sl = jnp.where(low, xl[b + 2], xl[b])
@@ -161,6 +162,10 @@
         parts = jnp.concatenate([xh[b + 1, g], xl[b + 1, g]], axis=0)
         v = jnp.dot(vv[...], parts, preferred_element_type=f32)
         new = x[b, g] + met[b, 0:1, :] * (acc[g] + v[:LEV] + v[LEV:])
+        if delta is not None:
+            extra = jnp.broadcast_to(delta[b, f : f + 1, :], (16, LANES))
+            tail = new[LEV - 16 :] + jnp.where(last, extra, 0.0)
+            new = jnp.concatenate([new[: LEV - 16], tail], axis=0)
         y[b, g] = new
         if yh is not None:
             hi, lo = split(new)
@@ -174,10 +179,9 @@
         g = slice((f + 1) * LEV - 16, (f + 1) * LEV)
         new = y[b, g] + jnp.where(last, jnp.broadcast_to(delta[b, f : f + 1, :], (16, LANES)), 0.0)
         y[b, g] = new
-        if yh is not None:
-            hi, lo = split(new)
-            yh[b + 1, g] = hi
-            yl[b + 1, g] = lo
+        hi, lo = split(new)
+        yh[b + 1, g] = hi
+        yl[b + 1, g] = lo
 
 
 def fold_edges(top, bottom):
@@ -233,17 +237,23 @@
     point_to[...] = table.T.astype(bf16)
 
 
-def pair_products(rows, wh, wl, out, transposed):
-    dims = (((1,), (1 if transposed else 0,)), ((), ()))
-
+def pair_products(rows, wc, out, transposed):
     def body(i, _):
         for k in range(16):
             j = i * 16 + k
             v = rows[pl.ds(j * 8, 8), :]
-            both = jnp.concatenate([v, v - v.astype(bf16).astype(f32)], axis=0).astype(bf16)
-            a = lax.dot_general(both, wh[j], dims, preferred_element_type=f32)
-            b = lax.dot_general(both, wl[j], dims, preferred_element_type=f32)
-            out[pl.ds(j * 8, 8), :] = a[:8] + a[8:] + b[:8]
+            hi = v.astype(bf16).astype(f32)
+            both = jnp.concatenate([hi, v - hi], axis=0).astype(bf16)
+            if transposed:
+                more = jnp.concatenate([hi, jnp.zeros_like(hi)], axis=0).astype(bf16)
+                lhs = jnp.concatenate([both, more], axis=1)
+                r = lax.dot_general(
+                    lhs, wc[j], (((1,), (1,)), ((), ())), preferred_element_type=f32
+                )
+                out[pl.ds(j * 8, 8), :] = r[:8] + r[8:]
+            else:
+                r = jnp.dot(both, wc[j], preferred_element_type=f32)
+                out[pl.ds(j * 8, 8), :] = r[:8, :BLK] + r[8:, :BLK] + r[:8, BLK:]
         return 0
 
     lax.fori_loop(0, PAIRS // 16, body, 0)
@@ -257,14 +267,14 @@
     nbr, metric, coef, stiff, coup, vert, owner, block, src,
     cell_nbr, cell_diff, overt, mask,
     st, x, xh, xl, y, yh, yl, vv, th, tl, met, cr, turned, near, delta, flux,
-    wt, wh, wl, rows_a, rows_b, slot_of, slot_to, point_of, point_to,
-    es, er, es2, er2, es3, er3,
+    wt, wc, rows_a, rows_b, slot_of, slot_to, point_of, point_to,
+    es, er, es2, er2,
     ids_s, ids_r, rep_s, rep_r, flx_s, flx_r, surf_s, surf_r, ofl_s, ofl_r,
     oe, ob,
     small_sem, st_sem, wt_sem, oc_sem, out_sem,
     ids_ss, ids_rs, rep_ss, rep_rs, flx_ss, flx_rs,
     surf_ss, surf_rs, ofl_ss, ofl_rs,
-    edge_ss, edge_rs, edge2_ss, edge2_rs, edge3_ss, edge3_rs, oh_ss, oh_rs,
+    edge_ss, edge_rs, edge2_ss, edge2_rs, oh_ss, oh_rs,
 ):
     c, d = lax.axis_index("comp"), lax.axis_index("dom")
     barrier = pltpu.get_barrier_semaphore()
@@ -309,7 +319,7 @@
             for f in range(FIELDS)
         ]
         state_in[0].start()
-        lax.fori_loop(1, DOM, hello, 0)
+        lax.fori_loop(1, DOM, hello, 0, unroll=True)
         greet(ocean_slab, d)
 
         @pl.when(cross_prev)
@@ -330,34 +340,18 @@
         weights_in.start()
 
         def exchange(out, into, send, recv):
-            def copy(i):
-                o = other(i)
-                return o, remote(out.at[o], into.at[d], send.at[o], recv.at[d], c, o)
-
             def start():
                 def body(i, _):
-                    copy(i)[1].start()
+                    o = other(i)
+                    remote(out.at[o], into.at[d], send, recv, c, o).start()
                     return 0
 
                 into[d] = out[d]
-                lax.fori_loop(1, DOM, body, 0)
-
-            def arrive():
-                def body(i, _):
-                    o = other(i)
-                    remote(out.at[o], into.at[o], send.at[o], recv.at[o], c, o).wait_recv()
-                    return 0
-
-                lax.fori_loop(1, DOM, body, 0)
-
-            def sent():
-                def body(i, _):
-                    copy(i)[1].wait_send()
-                    return 0
-
-                lax.fori_loop(1, DOM, body, 0)
-
-            return start, arrive, sent
+                lax.fori_loop(1, DOM, body, 0, unroll=True)
+
+            most = pl.ds(0, DOM - 1)
+            every = remote(out.at[most], into.at[most], send, recv, c, other(1))
+            return start, every.wait_recv, every.wait_send
 
         ids_start, ids_arrive, ids_sent = exchange(ids_s, ids_r, ids_ss, ids_rs)
         rep_start, rep_arrive, rep_sent = exchange(rep_s, rep_r, rep_ss, rep_rs)
@@ -403,34 +397,25 @@
         edge2_start, edge2_arrive, edge2_sent = edge_copies(
             es2, er2, edge2_ss, edge2_rs, pl.ds(0, ROWS)
         )
-        edge3_start, edge3_arrive, edge3_sent = edge_copies(
-            es3, er3, edge3_ss, edge3_rs, pl.ds(0, 8)
-        )
 
         @pl.when(jnp.logical_not(has_prev))
         def _():
             er[0] = jnp.zeros((ROWS, 128), f32)
             er2[0] = jnp.zeros((ROWS, 128), f32)
-            er3[0] = jnp.zeros((8, 128), f32)
 
         @pl.when(jnp.logical_not(has_next))
         def _():
             er[1] = jnp.zeros((ROWS, 128), f32)
             er2[1] = jnp.zeros((ROWS, 128), f32)
-            er3[1] = jnp.zeros((8, 128), f32)
-
-        state_in[0].wait()
-        pack(0, st, x, xh, xl)
-        edges_out(0, x, es)
+
         for copy in small_in:
             copy.wait()
         pair_tables(owner, block, src, slot_of, slot_to, point_of, point_to, ids_s)
         pl.semaphore_wait(
             barrier, DOM + jnp.where(cross_prev, 1, 0) + jnp.where(cross_next, 1, 0)
         )
-        edges[0][0]()
         ids_start()
-        for f in range(1, FIELDS):
+        for f in range(FIELDS):
             state_in[f].wait()
             pack(f, st, x, xh, xl)
             edges_out(f, x, es)
@@ -462,42 +447,25 @@
 
         def halves(j, _):
             hi, lo = split(wt[j])
-            wh[j] = hi
-            wl[j] = lo
+            wc[j, :, :BLK] = hi
+            wc[j, :, BLK:] = lo
             return 0
 
         lax.fori_loop(0, PAIRS, halves, 0, unroll=2)
 
-        def first(i, _):
-            @pl.when(i == 4)
-            def _():
-                for f in range(FIELDS):
-                    edges[f][1]()
-                edges_in(er, xh, xl)
-
-            @pl.when(i == 6)
-            def _():
-                for f in range(FIELDS):
-                    edges_out(f, y, es2)
-                edge2_start()
-
-            edge = jnp.where(i == 4, 0, BLOCKS - 1)
-            b = jnp.where(i < 4, i + 1, jnp.where(i < 6, edge, i - 1))
+        for b in (1, 2, 3, 4):
             advance(b, x, xh, xl, y, yh, yl, vv, th, tl, met)
-            return 0
-
-        lax.fori_loop(0, BLOCKS, first, 0)
 
         rep_arrive()
         rows_a[...] = pick_rows(slot_to[...], rep_r[...].reshape(256, BLK))
-        pair_products(rows_a, wh, wl, rows_b, True)
+        pair_products(rows_a, wc, rows_b, True)
         surface = pick_rows(point_of[...], rows_b[...])
         top = jnp.concatenate(
             [st[f * 2048 + 2032 : f * 2048 + 2048, :] for f in range(FIELDS)], axis=0
         )
         fl = jnp.concatenate([coef[...]] * FIELDS, axis=0) * (top - surface)
         rows_a[...] = pick_rows(point_to[...], fl)
-        pair_products(rows_a, wh, wl, rows_b, False)
+        pair_products(rows_a, wc, rows_b, False)
         flx_s[...] = pick_rows(slot_of[...], rows_b[...]).reshape(DOM, 8, BLK)
         flx_start()
 
@@ -507,61 +475,50 @@
             w = to_blocks([flux[pl.ds(h * 8 + q, 8, stride=NPTS), :] for q in range(8)])
             for b in range(BLOCKS):
                 delta[b, :, h * 128 : (h + 1) * 128] = w[b]
-        es3[0], es3[1] = fold_edges(delta[BLOCKS - 1], delta[0])
-        edge3_start()
-
-        def surface_term(b, _):
+        for b in (1, 2, 3, 4):
             add_surface(b, delta, y, yh, yl)
-            return 0
-
-        lax.fori_loop(0, BLOCKS, surface_term, 0)
+        for f in range(FIELDS):
+            edges[f][1]()
+        edges_in(er, xh, xl)
+        for b in (0, 7):
+            advance(b, x, xh, xl, y, yh, yl, vv, th, tl, met, delta)
+        for f in range(FIELDS):
+            edges_out(f, y, es2)
+        edge2_start()
+        for b in (5, 6):
+            advance(b, x, xh, xl, y, yh, yl, vv, th, tl, met, delta)
 
         def block_out(b):
             return pltpu.make_async_copy(x.at[b], packed_hbm.at[b], out_sem.at[b])
 
-        def second(i, _):
-            @pl.when(i == 3)
-            def _():
-                flx_arrive()
-
-                def gather(j, accs):
-                    which, val = ids_r[j], flx_r[j]
-                    return tuple(
-                        acc + jnp.where(which == b, val, 0.0) for b, acc in enumerate(accs)
-                    )
-
-                zero = jnp.zeros((8, BLK), f32)
-                accs = lax.fori_loop(0, DOM, gather, (zero,) * OBLOCKS, unroll=4)
-                for b in range(OBLOCKS):
-                    ofl_s[:, b * BLK : (b + 1) * BLK] = accs[b]
-                remote(ofl_s, ofl_r.at[c], ofl_ss, ofl_rs.at[c], ocean_slab, d).start()
-
-            @pl.when(i == BLOCKS - 2)
-            def _():
-                edge2_arrive()
-                edge3_arrive()
-                last = iota((16, 128), 0) == 15
-                for side in range(2):
-                    for f in range(FIELDS):
-                        g = slice((f + 1) * LEV - 16, (f + 1) * LEV)
-                        extra = jnp.broadcast_to(er3[side, f : f + 1, :], (16, 128))
-                        er2[side, g] = er2[side, g] + jnp.where(last, extra, 0.0)
-                edges_in(er2, yh, yl)
-
-            b = jnp.where(i < BLOCKS - 2, i + 1, (i - (BLOCKS - 2)) * (BLOCKS - 1))
-            advance(b, y, yh, yl, x, None, None, vv, th, tl, met)
-            add_surface(b, delta, x, None, None)
-            block_out(b).start()
-            return 0
-
-        lax.fori_loop(0, BLOCKS, second, 0)
+        def second(blocks):
+            for b in blocks:
+                advance(b, y, yh, yl, x, None, None, vv, th, tl, met, delta)
+            for b in blocks:
+                block_out(b).start()
+
+        second((1, 2))
+        flx_arrive()
+
+        def gather(j, accs):
+            which, val = ids_r[j], flx_r[j]
+            return tuple(acc + jnp.where(which == b, val, 0.0) for b, acc in enumerate(accs))
+
+        zero = jnp.zeros((8, BLK), f32)
+        accs = lax.fori_loop(0, DOM, gather, (zero,) * OBLOCKS, unroll=4)
+        for b in range(OBLOCKS):
+            ofl_s[:, b * BLK : (b + 1) * BLK] = accs[b]
+        remote(ofl_s, ofl_r.at[c], ofl_ss, ofl_rs.at[c], ocean_slab, d).start()
+        second((3, 4, 5, 6))
+        edge2_arrive()
+        edges_in(er2, yh, yl)
+        second((0, 7))
         ids_sent()
         rep_sent()
         flx_sent()
         for f in range(FIELDS):
             edges[f][2]()
         edge2_sent()
-        edge3_sent()
         remote(ofl_s, ofl_r.at[c], ofl_ss, ofl_rs.at[c], ocean_slab, d).wait_send()
         for b in range(BLOCKS):
             block_out(b).wait()
@@ -683,41 +640,49 @@
 
 def finish(packed_hbm, ocean_hbm, atm_hbm, ocean_out_hbm, x, st, blank, in_sem, out_sem, oc_sem):
     c = lax.axis_index("comp")
+    parts, levels = 8, ROWS // 8
+    rows = levels * NPTS
     outs = [
         pltpu.make_async_copy(
-            st.at[pl.ds(f * 2048, 2048)], atm_hbm.at[pl.ds(f * 2048, 2048)], out_sem.at[f]
-        )
-        for f in range(FIELDS)
+            st.at[pl.ds(i * rows, rows)], atm_hbm.at[pl.ds(i * rows, rows)], out_sem.at[i]
+        )
+        for i in range(parts)
     ]
 
     @pl.when(c < ATM)
     def _():
         ins = [
             pltpu.make_async_copy(
-                packed_hbm.at[:, pl.ds(f * LEV, LEV)], x.at[:, pl.ds(f * LEV, LEV)], in_sem.at[f]
+                packed_hbm.at[:, pl.ds(i * levels, levels)],
+                x.at[:, pl.ds(i * levels, levels)],
+                in_sem.at[i],
             )
-            for f in range(FIELDS)
+            for i in range(parts)
         ]
         for copy in ins:
             copy.start()
         blank[...] = jnp.zeros((OROWS, CELLS), f32)
         zero_out = pltpu.make_async_copy(blank, ocean_out_hbm, oc_sem)
-        zero_out.start()
-        for f in range(FIELDS):
-            ins[f].wait()
-            unpack(f, x, st)
-            outs[f].start()
+        for i in range(parts):
+            ins[i].wait()
+            unpack(i * levels, levels, x, st)
+            outs[i].start()
+            if i == 2:
+                zero_out.start()
         zero_out.wait()
         for copy in outs:
             copy.wait()
 
     @pl.when(c == ATM)
     def _():
-        ocean_out = pltpu.make_async_copy(ocean_hbm, ocean_out_hbm, oc_sem)
+        ocean_in = pltpu.make_async_copy(ocean_hbm, blank, in_sem.at[0])
+        ocean_in.start()
+        for i in range(parts):
+            st[i * rows : (i + 1) * rows] = jnp.zeros((rows, ELEMS), f32)
+            outs[i].start()
+        ocean_in.wait()
+        ocean_out = pltpu.make_async_copy(blank, ocean_out_hbm, oc_sem)
         ocean_out.start()
-        for f in range(FIELDS):
-            st[f * 2048 : (f + 1) * 2048] = jnp.zeros((2048, ELEMS), f32)
-            outs[f].start()
         ocean_out.wait()
         for copy in outs:
             copy.wait()
@@ -745,22 +710,20 @@
         vmem((BLOCKS, 2 * LANES, LANES), bf16), vmem((BLOCKS, 8, LANES), f32),
         vmem((5, NPTS, LANES), f32), vmem((5, NPTS, LANES), f32), vmem((BLOCKS, 8, 128), i32),
         vmem((BLOCKS, 8, LANES), f32), vmem((128, BLK), f32),
-        vmem((PAIRS, BLK, BLK), f32), vmem((PAIRS, BLK, BLK), bf16), vmem((PAIRS, BLK, BLK), bf16),
+        vmem((PAIRS, BLK, BLK), f32), vmem((PAIRS, BLK, 2 * BLK), bf16),
         vmem((256, BLK), f32), vmem((256, BLK), f32),
         vmem((256, 256), bf16), vmem((256, 256), bf16), vmem((64, 256), bf16), vmem((256, 64), bf16),
         vmem((2, ROWS, 128), f32), vmem((2, ROWS, 128), f32),
         vmem((2, ROWS, 128), f32), vmem((2, ROWS, 128), f32),
-        vmem((2, 8, 128), f32), vmem((2, 8, 128), f32),
         vmem(message, i32), vmem(message, i32), vmem(message, f32), vmem(message, f32),
         vmem(message, f32), vmem(message, f32),
         vmem((8, CELLS), f32), vmem((8, CELLS), f32), vmem((8, CELLS), f32),
         vmem((ATM, 8, CELLS), f32),
         vmem((OROWS, CELLS + 2 * BLK), f32), vmem((OROWS, CELLS), f32),
         sem((9,)), sem((FIELDS,)), sem, sem, sem((BLOCKS,)),
-        sem((DOM,)), sem((DOM,)), sem((DOM,)), sem((DOM,)), sem((DOM,)), sem((DOM,)),
+        sem, sem, sem, sem, sem, sem,
         sem((ATM,)), sem, sem, sem((ATM,)),
         sem((FIELDS, 2)), sem((FIELDS, 2)), sem((2,)), sem((2,)), sem((2,)), sem((2,)),
-        sem((2,)), sem((2,)),
     ]
     packed, ocean = pl.pallas_call(
         kernel,
@@ -791,7 +754,7 @@
         out_specs=(anywhere, anywhere),
         scratch_shapes=[
             vmem(big, f32), vmem((FIELDS * 2048, ELEMS), f32), vmem((OROWS, CELLS), f32),
-            sem((FIELDS,)), sem((FIELDS,)), sem,
+            sem((8,)), sem((8,)), sem,
         ],
         compiler_params=pltpu.CompilerParams(vmem_limit_bytes=60 << 20),
         name="finish",

time: 76.9 us -> 37.4 us (0.49)
  the two profiles are of different devices: /device:TPU:6 before, /device:TPU:2 now
where the time goes in v2:
time: 37.4 us; the launch traced here: 36.9 us
  Pallas kernels  36.3 us (97%)
  between operations  0.64 us (2%)
    pallas_call x1, Pallas kernels, local(): pl.pallas_call(kernel, out_shape=(jax.ShapeDtypeStruct(big, f32), jax.Sha...  32.1 us
    pallas_call x1, Pallas kernels, local(): pl.pallas_call(finish, out_shape=(jax.ShapeDtypeStruct((FIELDS * 2048, EL...  4.15 us

profile of v2, /device:TPU:2, one launch (start us, length us, event | category | flops | bytes accessed | tf_op | source)
XLA Modules:
  0.0 36.9 jit_solution(767281966588834151)
XLA Ops:
  0.6 32.1 %coupled_step.1 = (f32[8,512,256]{2,1,0:T(8,128)}, f32[320,1024]{1,0:T(8,128)}) custom-call(f32[8192,128]{1,0:T(8,128)} %bitcast.11, f32[32,128,128]{2,1,0:T(8,128)} %bitcast.12, f32[320,1024]{1,0:T(8,128)} %bitcast.13, s32[4,128]{1,0:T(4,128)} %bitcast.18, f32[16,128]{1,0:T(8,128)} %bitcast.16, f32[16,128]{1,0:T(8,128)} %bitcast.17, f32[16,16]{1,0:T(8,128)} %stiff_h.1, ...), custom_call_target="tpu_custom_call" | custom-call | tf_op jit(solution)/shard_map/coupled_step/pallas_call | solution.py:728
  32.8 4.2 %finish.1 = (f32[8192,128]{1,0:T(8,128)}, f32[320,1024]{1,0:T(8,128)}) custom-call(f32[8,512,256]{2,1,0:T(8,128)} %get-tuple-element.6.packed_hbm, f32[320,1024]{1,0:T(8,128)} %get-tuple-element.7.ocean_hbm), custom_call_target="tpu_custom_call" | custom-call | tf_op jit(solution)/shard_map/finish/pallas_call | solution.py:747

commit v3 on v2

--- a/solution.py
+++ b/solution.py
@@ -69,7 +69,7 @@
                 xl[b + 1, pl.ds(row, 16), cols] = lo
         return 0
 
-    lax.fori_loop(0, LEV // 16, body, 0, unroll=2)
+    lax.fori_loop(0, LEV // 16, body, 0, unroll=4)
 
 
 def unpack(first, levels, x, st):
@@ -82,7 +82,7 @@
                 st[pl.ds(row * NPTS + h * 8 + q, 16, stride=NPTS), :] = w[q]
         return 0
 
-    lax.fori_loop(0, levels // 16, body, 0, unroll=2)
+    lax.fori_loop(0, levels // 16, body, 0, unroll=4)
 
 
 def small_tables(first, nbr, metric, stiff, coup, vert, cr, met, near, vv):
@@ -419,15 +419,6 @@
             state_in[f].wait()
             pack(f, st, x, xh, xl)
             edges_out(f, x, es)
-            edges[f][0]()
-
-        small_tables(c * (DOM * ELEMS) + d * ELEMS, nbr, metric, stiff, coup, vert, cr, met, near, vv)
-
-        def table(b, _):
-            operator_block(b, near, cr, turned, th, tl)
-            return 0
-
-        lax.fori_loop(0, BLOCKS, table, 0)
 
         remote(surf_s, surf_r, surf_ss.at[0], surf_rs, ocean_slab, d).wait_recv()
         ids_arrive()
@@ -442,6 +433,17 @@
 
         lax.fori_loop(0, DOM, answer, 0, unroll=4)
         rep_start()
+        for f in range(FIELDS):
+            edges[f][0]()
+
+        small_tables(c * (DOM * ELEMS) + d * ELEMS, nbr, metric, stiff, coup, vert, cr, met, near, vv)
+
+        def table(b, _):
+            operator_block(b, near, cr, turned, th, tl)
+            return 0
+
+        lax.fori_loop(0, BLOCKS, table, 0)
+
 
         weights_in.wait()
 
@@ -612,18 +614,29 @@
             return 0
 
         lax.fori_loop(0, OBLOCKS, cells, 0)
+        sea = mask[...] == 1
+        done = []
+        for f in range(FIELDS):
+            g = slice(f * OLEV, (f + 1) * OLEV)
+            ob[g, :] = jnp.where(sea, ob[g, :], oe[g, BLK : BLK + CELLS])
+            rest = pl.ds(f * OLEV + 8, OLEV - 8)
+            done.append(pltpu.make_async_copy(ob.at[rest], ocean_out_hbm.at[rest], out_sem.at[f]))
+            done[-1].start()
         for comp in range(ATM):
             remote(ofl_s, ofl_r.at[comp], ofl_ss, ofl_rs.at[comp], comp, d).wait_recv()
         total = ofl_r[0] + ofl_r[1] + ofl_r[2]
         total = 0.5 * (total[:4] + total[4:])
-        sea = mask[...] == 1
-        first_row = iota((OLEV, CELLS), 0) == 0
+        wet_top = (iota((8, CELLS), 0) == 0) & sea
         for f in range(FIELDS):
-            g = slice(f * OLEV, (f + 1) * OLEV)
-            fresh = ob[g, :] + jnp.where(first_row, total[f : f + 1, :], 0.0)
-            ob[g, :] = jnp.where(sea, fresh, oe[g, BLK : BLK + CELLS])
-        ocean_done = pltpu.make_async_copy(ob, ocean_out_hbm, out_sem.at[0])
-        ocean_done.start()
+            g = slice(f * OLEV, f * OLEV + 8)
+            ob[g, :] = ob[g, :] + jnp.where(wet_top, total[f : f + 1, :], 0.0)
+            first = pl.ds(f * OLEV, 8)
+            done.append(
+                pltpu.make_async_copy(
+                    ob.at[first], ocean_out_hbm.at[first], out_sem.at[FIELDS + f]
+                )
+            )
+            done[-1].start()
         for copy in surf_out:
             copy.wait_send()
 
@@ -635,7 +648,8 @@
         def _():
             down.wait_send()
 
-        ocean_done.wait()
+        for copy in done:
+            copy.wait()
 
 
 def finish(packed_hbm, ocean_hbm, atm_hbm, ocean_out_hbm, x, st, blank, in_sem, out_sem, oc_sem):

time: 37.4 us -> 36.4 us (0.973)
  Pallas kernels: 36.3 us -> 35.1 us
    pallas_call x1, Pallas kernels: 32.1 us -> 31.3 us  [local(): pl.pallas_call(kernel, out_shape=(jax.ShapeDtypeStruct(big, f32), jax.Sha...]
where the time goes in v3:
time: 36.4 us; the launch traced here: 35.8 us
  Pallas kernels  35.1 us (96%)
  between operations  0.64 us (2%)
    pallas_call x1, Pallas kernels, local(): pl.pallas_call(kernel, out_shape=(jax.ShapeDtypeStruct(big, f32), jax.Sha...  31.3 us
    pallas_call x1, Pallas kernels, local(): pl.pallas_call(finish, out_shape=(jax.ShapeDtypeStruct((FIELDS * 2048, EL...  3.86 us

profile of v3, /device:TPU:2, one launch (start us, length us, event | category | flops | bytes accessed | tf_op | source)
XLA Modules:
  0.0 35.8 jit_solution(13244423207133675696)
XLA Ops:
  0.6 31.3 %coupled_step.1 = (f32[8,512,256]{2,1,0:T(8,128)}, f32[320,1024]{1,0:T(8,128)}) custom-call(f32[8192,128]{1,0:T(8,128)} %bitcast.11, f32[32,128,128]{2,1,0:T(8,128)} %bitcast.12, f32[320,1024]{1,0:T(8,128)} %bitcast.13, s32[4,128]{1,0:T(4,128)} %bitcast.18, f32[16,128]{1,0:T(8,128)} %bitcast.16, f32[16,128]{1,0:T(8,128)} %bitcast.17, f32[16,16]{1,0:T(8,128)} %stiff_h.1, ...), custom_call_target="tpu_custom_call" | custom-call | tf_op jit(solution)/shard_map/coupled_step/pallas_call | solution.py:742
  31.9 3.9 %finish.1 = (f32[8192,128]{1,0:T(8,128)}, f32[320,1024]{1,0:T(8,128)}) custom-call(f32[8,512,256]{2,1,0:T(8,128)} %get-tuple-element.6.packed_hbm, f32[320,1024]{1,0:T(8,128)} %get-tuple-element.7.ocean_hbm), custom_call_target="tpu_custom_call" | custom-call | tf_op jit(solution)/shard_map/finish/pallas_call | solution.py:761

commit v4 on v3

--- a/solution.py
+++ b/solution.py
@@ -477,8 +477,6 @@
             w = to_blocks([flux[pl.ds(h * 8 + q, 8, stride=NPTS), :] for q in range(8)])
             for b in range(BLOCKS):
                 delta[b, :, h * 128 : (h + 1) * 128] = w[b]
-        for b in (1, 2, 3, 4):
-            add_surface(b, delta, y, yh, yl)
         for f in range(FIELDS):
             edges[f][1]()
         edges_in(er, xh, xl)
@@ -487,6 +485,8 @@
         for f in range(FIELDS):
             edges_out(f, y, es2)
         edge2_start()
+        for b in (1, 2, 3, 4):
+            add_surface(b, delta, y, yh, yl)
         for b in (5, 6):
             advance(b, x, xh, xl, y, yh, yl, vv, th, tl, met, delta)
 

time: 36.4 us -> 36.4 us (level)
  no operation moved by 1% of the time
where the time goes in v4:
time: 36.4 us; the launch traced here: 35.7 us
  Pallas kernels  35.1 us (96%)
  between operations  0.64 us (2%)
    pallas_call x1, Pallas kernels, local(): pl.pallas_call(kernel, out_shape=(jax.ShapeDtypeStruct(big, f32), jax.Sha...  31.2 us
    pallas_call x1, Pallas kernels, local(): pl.pallas_call(finish, out_shape=(jax.ShapeDtypeStruct((FIELDS * 2048, EL...  3.86 us

profile of v4, /device:TPU:2, one launch (start us, length us, event | category | flops | bytes accessed | tf_op | source)
XLA Modules:
  0.0 35.7 jit_solution(3761275490694422056)
XLA Ops:
  0.6 31.2 %coupled_step.1 = (f32[8,512,256]{2,1,0:T(8,128)}, f32[320,1024]{1,0:T(8,128)}) custom-call(f32[8192,128]{1,0:T(8,128)} %bitcast.11, f32[32,128,128]{2,1,0:T(8,128)} %bitcast.12, f32[320,1024]{1,0:T(8,128)} %bitcast.13, s32[4,128]{1,0:T(4,128)} %bitcast.18, f32[16,128]{1,0:T(8,128)} %bitcast.16, f32[16,128]{1,0:T(8,128)} %bitcast.17, f32[16,16]{1,0:T(8,128)} %stiff_h.1, ...), custom_call_target="tpu_custom_call" | custom-call | tf_op jit(solution)/shard_map/coupled_step/pallas_call | solution.py:742
  31.9 3.9 %finish.1 = (f32[8192,128]{1,0:T(8,128)}, f32[320,1024]{1,0:T(8,128)}) custom-call(f32[8,512,256]{2,1,0:T(8,128)} %get-tuple-element.6.packed_hbm, f32[320,1024]{1,0:T(8,128)} %get-tuple-element.7.ocean_hbm), custom_call_target="tpu_custom_call" | custom-call | tf_op jit(solution)/shard_map/finish/pallas_call | solution.py:761
